TPU v7x, 32 devices: a whole 2x2x4 slice. The times are simulated.
32 devices in a mesh: row: 4 (over z), col: 8 (over y, x, core).
Axes of the slice: x: 2, y: 2, z: 4, core: 2. Of those that a mesh axis runs over, the one named last changes fastest.
Arguments:
- region: float32 [8, 1024, 8, 1024], P(None, 'col', None, 'row'), may hold values from -6 to 6
- l_panels: bfloat16 [3, 1024, 11, 1024], P(None, 'col', None, 'row'), may hold values from -0.0625 to 0.0625
- u_panels: bfloat16 [3, 11, 1024, 1024], P(None, None, 'col', 'row'), may hold values from -0.0625 to 0.0625
- diag_inv: float32 [3, 1024, 1024], P(None, 'col', 'row'), may hold values from -6 to 6
- pattern: int32 [3, 11, 8], replicated, may hold values from 0 to 1, as said below
Outputs:
- inverse: float32 [11, 1024, 11, 1024], P(None, 'col', None, 'row')
Inputs may be any that keep to these rules, and one draw needn't show every extreme that they name: pattern[s] marks the 128-row blocks in the structure of supernode s: only blocks of segments after s; for the last supernode only blocks of the ancestor region; for every other supernode all blocks of one later supernode (its parent in the elimination tree) and otherwise only blocks that the parent's pattern also marks.
All inputs are finite; a program needn't handle non-finite values.
Results may differ from a plain program's by a relative error of at most 0.0003.
Values may be sent and summed in bfloat16 or wider, within the bound.
A program may use at most 128 MiB of HBM per device.

v0:
```python
import jax
import jax.numpy as jnp
from jax import lax
from jax.sharding import PartitionSpec as P

BLK = 128
NSUP = 3
NSEG = 11


def per_device(region, l_panels, u_panels, diag_inv, pattern):
    rows_here = region.shape[1]
    cols_here = region.shape[3]
    row_index = lax.axis_index("row")
    col_index = lax.axis_index("col")
    block_mask = jnp.repeat(pattern.astype(jnp.float32), BLK, axis=2)
    mask_rows = lax.dynamic_slice_in_dim(block_mask, col_index * rows_here, rows_here, 2)
    mask_cols = lax.dynamic_slice_in_dim(block_mask, row_index * cols_here, cols_here, 2)
    inverse = jnp.zeros((NSEG, rows_here, NSEG, cols_here), jnp.float32)
    inverse = inverse.at[NSUP:, :, NSUP:, :].set(region)
    for level in reversed(range(NSUP)):
        start_seg = level + 1
        lower = l_panels[level][:, start_seg:, :] * mask_cols[level, None, start_seg:, :].astype(
            jnp.bfloat16
        )
        lower_full = lax.all_gather(lower, "col", axis=0, tiled=True).astype(jnp.float32)
        upper = u_panels[level][start_seg:] * mask_rows[level, start_seg:, :, None].astype(
            jnp.bfloat16
        )
        upper_full = lax.all_gather(upper, "row", axis=2, tiled=True).astype(jnp.float32)
        known = inverse[start_seg:, :, start_seg:, :]
        col_terms = jnp.einsum("ajbk,wbk->ajw", known, lower_full, precision=lax.Precision.HIGHEST)
        col_sum = lax.psum_scatter(col_terms, "row", scatter_dimension=2, tiled=True)
        column = -mask_rows[level, start_seg:, :, None] * col_sum
        row_terms = jnp.einsum("akw,akbj->wbj", upper_full, known, precision=lax.Precision.HIGHEST)
        diag_terms = jnp.einsum("akw,akv->wv", upper_full, column, precision=lax.Precision.HIGHEST)
        row_sum, diag_sum = (
            lax.psum_scatter(row_terms, "col", scatter_dimension=0, tiled=True),
            lax.psum_scatter(diag_terms, "col", scatter_dimension=0, tiled=True),
        )
        row_panel = -mask_cols[level, None, start_seg:, :] * row_sum
        diagonal = diag_inv[level] - diag_sum
        inverse = inverse.at[start_seg:, :, level, :].set(column)
        inverse = inverse.at[level, :, start_seg:, :].set(row_panel)
        inverse = inverse.at[level, :, level, :].set(diagonal)
    return inverse


def solution(mesh):
    in_specs = (
        P(None, "col", None, "row"),
        P(None, "col", None, "row"),
        P(None, None, "col", "row"),
        P(None, "col", "row"),
        P(),
    )
    out_specs = P(None, "col", None, "row")
    return jax.shard_map(
        per_device, mesh=mesh, in_specs=in_specs, out_specs=out_specs, check_vma=False
    )
```

profile of v0, /device:TPU:0, one launch (start us, length us, event | category | flops | bytes accessed | tf_op | source)
XLA Modules:
  0.0 914.5 jit_solution(10235350321088960267)
XLA Ops:
  12.6 37.0 %all-gather.7.cloned.1.call-done = bf16[1024,8,256]{2,0,1:T(8,128)(2,1)} async-done(((bf16[128,8,256]{2,0,1:T(8,128)(2,1)}), bf16[1024,8,256]{2,0,1:T(8,128)(2,1)}) %all-gather.7.cloned.1.call-update) | async-done | bytes 4194320 | tf_op jit(solution)/shard_map/all_gather | solution.py:26
  49.7 19.4 %fusion.29 = f32[8,128,1024]{1,2,0:T(8,128)} fusion(bf16[1024,8,256]{2,0,1:T(8,128)(2,1)} %all-gather.7.cloned.1.call-done, f32[8,128,8,256]{3,2,1,0:T(8,128)} %param.25), kind=kOutput, calls=%fused_computation.19 | convolution fusion | flops 25769803776 | bytes 16777216 | tf_op jit(solution)/shard_map/ajbk,wbk->ajw/dot_general | solution.py:32
  69.6 27.3 %all-gather.9.cloned.1.call-done = bf16[8,128,1024]{1,2,0:T(8,128)(2,1)} async-done(((bf16[8,128,256]{1,2,0:T(8,128)(2,1)}), bf16[8,128,1024]{1,2,0:T(8,128)(2,1)}) %all-gather.9.cloned.1.call-update) | async-done | bytes 2097168 | tf_op jit(solution)/shard_map/all_gather | solution.py:30
  96.9 18.6 %fusion.18 = f32[1024,8,256]{2,0,1:T(8,128)} fusion(f32[8,128,8,256]{3,2,1,0:T(8,128)} %param.25, bf16[8,128,1024]{1,2,0:T(8,128)(2,1)} %all-gather.9.cloned.1.call-done), kind=kOutput, calls=%fused_computation.14 | convolution fusion | flops 25769803776 | bytes 18874368 | tf_op jit(solution)/shard_map/akw,akbj->wbj/dot_general | solution.py:35
  116.6 58.3 %reduce-scatter.10.cloned.1.call-done = f32[8,128,256]{1,2,0:T(8,128)} async-done(((f32[8,128,1024]{1,2,0:T(8,128)}), f32[8,128,256]{1,2,0:T(8,128)}) %reduce-scatter.10.cloned.1.call-update) | async-done | bytes 1048592 | tf_op jit(solution)/shard_map/reduce_scatter | solution.py:33
  184.2 6.7 copy.28
  191.8 6.4 scatter.34
  199.7 50.4 %reduce-scatter.12.cloned.1.call-done = f32[128,8,256]{2,0,1:T(8,128)} async-done(((f32[1024,8,256]{2,0,1:T(8,128)}), f32[128,8,256]{2,0,1:T(8,128)}) %reduce-scatter.12.cloned.1.call-update) | async-done | bytes 1048592 | tf_op jit(solution)/shard_map/reduce_scatter | solution.py:38
  252.4 36.8 %reduce-scatter.14.cloned.1.call-done = f32[128,256]{1,0:T(8,128)} async-done(((f32[1024,256]{1,0:T(8,128)}), f32[128,256]{1,0:T(8,128)}) %reduce-scatter.14.cloned.1.call-update) | async-done | bytes 131088 | tf_op jit(solution)/shard_map/reduce_scatter | solution.py:39
  290.7 39.0 %all-gather.11.cloned.1.call-done = bf16[1024,9,256]{2,0,1:T(8,128)(2,1)} async-done(((bf16[128,9,256]{2,0,1:T(8,128)(2,1)}), bf16[1024,9,256]{2,0,1:T(8,128)(2,1)}) %all-gather.11.cloned.1.call-update) | async-done | bytes 4718608 | tf_op jit(solution)/shard_map/all_gather | solution.py:26
  329.7 21.6 %fusion.26 = f32[9,128,1024]{2,1,0:T(8,128)} fusion(f32[11,128,11,256]{3,1,2,0:T(8,128)} %bitcast_dynamic-update-slice_fusion.6, bf16[1024,9,256]{2,0,1:T(8,128)(2,1)} %all-gather.11.cloned.1.call-done), kind=kOutput, calls=%fused_computation.18 | convolution fusion | flops 32614907904 | bytes 25296896 | tf_op jit(solution)/shard_map/ajbk,wbk->ajw/dot_general | solution.py:32
  351.6 29.7 %all-gather.13.cloned.1.call-done = bf16[9,128,1024]{1,2,0:T(8,128)(2,1)} async-done(((bf16[9,128,256]{1,2,0:T(8,128)(2,1)}), bf16[9,128,1024]{1,2,0:T(8,128)(2,1)}) %all-gather.13.cloned.1.call-update) | async-done | bytes 2359312 | tf_op jit(solution)/shard_map/all_gather | solution.py:30
  381.3 23.5 %fusion.15 = f32[1024,9,256]{2,0,1:T(8,128)} fusion(f32[11,128,11,256]{3,1,2,0:T(8,128)} %bitcast_dynamic-update-slice_fusion.6, bf16[9,128,1024]{1,2,0:T(8,128)(2,1)} %all-gather.13.cloned.1.call-done), kind=kOutput, calls=%fused_computation.13 | convolution fusion | flops 32614907904 | bytes 22413312 | tf_op jit(solution)/shard_map/akw,akbj->wbj/dot_general | solution.py:35
  405.7 62.0 %reduce-scatter.16.cloned.1.call-done = f32[9,128,256]{2,1,0:T(8,128)} async-done(((f32[9,128,1024]{2,1,0:T(8,128)}), f32[9,128,256]{2,1,0:T(8,128)}) %reduce-scatter.16.cloned.1.call-update) | async-done | bytes 1179664 | tf_op jit(solution)/shard_map/reduce_scatter | solution.py:33
  480.3 68.0 %reduce-scatter.18.cloned.1.call-done = f32[128,9,256]{2,0,1:T(8,128)} async-done(((f32[1024,9,256]{2,0,1:T(8,128)}), f32[128,9,256]{2,0,1:T(8,128)}) %reduce-scatter.18.cloned.1.call-update) | async-done | bytes 1179664 | tf_op jit(solution)/shard_map/reduce_scatter | solution.py:38
  550.7 36.6 %reduce-scatter.20.cloned.1.call-done = f32[128,256]{1,0:T(8,128)} async-done(((f32[1024,256]{1,0:T(8,128)}), f32[128,256]{1,0:T(8,128)}) %reduce-scatter.20.cloned.1.call-update) | async-done | bytes 131088 | tf_op jit(solution)/shard_map/reduce_scatter | solution.py:39
  588.9 41.4 %all-gather.15.cloned.1.call-done = bf16[1024,10,256]{2,0,1:T(8,128)(2,1)} async-done(((bf16[128,10,256]{2,0,1:T(8,128)(2,1)}), bf16[1024,10,256]{2,0,1:T(8,128)(2,1)}) %all-gather.15.cloned.1.call-update) | async-done | bytes 5242896 | tf_op jit(solution)/shard_map/all_gather | solution.py:26
  630.3 25.7 %fusion.22 = f32[10,128,1024]{2,1,0:T(8,128)} fusion(f32[11,128,11,256]{3,1,2,0:T(8,128)} %bitcast_dynamic-update-slice_fusion.5, bf16[1024,10,256]{2,0,1:T(8,128)(2,1)} %all-gather.15.cloned.1.call-done), kind=kOutput, calls=%fused_computation.16 | convolution fusion | flops 40265318400 | bytes 26345472 | tf_op jit(solution)/shard_map/ajbk,wbk->ajw/dot_general | solution.py:32
  656.2 30.2 %all-gather.17.cloned.1.call-done = bf16[10,128,1024]{1,2,0:T(8,128)(2,1)} async-done(((bf16[10,128,256]{1,2,0:T(8,128)(2,1)}), bf16[10,128,1024]{1,2,0:T(8,128)(2,1)}) %all-gather.17.cloned.1.call-update) | async-done | bytes 2621456 | tf_op jit(solution)/shard_map/all_gather | solution.py:30
  686.5 29.9 %fusion.12 = f32[1024,10,256]{2,0,1:T(8,128)} fusion(f32[11,128,11,256]{3,1,2,0:T(8,128)} %bitcast_dynamic-update-slice_fusion.5, bf16[10,128,1024]{1,2,0:T(8,128)(2,1)} %all-gather.17.cloned.1.call-done), kind=kOutput, calls=%fused_computation.12 | convolution fusion | flops 40265318400 | bytes 26214400 | tf_op jit(solution)/shard_map/akw,akbj->wbj/dot_general | solution.py:35
  717.1 64.2 %reduce-scatter.22.cloned.1.call-done = f32[10,128,256]{2,1,0:T(8,128)} async-done(((f32[10,128,1024]{2,1,0:T(8,128)}), f32[10,128,256]{2,1,0:T(8,128)}) %reduce-scatter.22.cloned.1.call-update) | async-done | bytes 1310736 | tf_op jit(solution)/shard_map/reduce_scatter | solution.py:33
  781.3 5.6 convolution_bitcast_fusion
  791.1 75.8 %reduce-scatter.24.cloned.1.call-done = f32[128,10,256]{2,0,1:T(8,128)} async-done(((f32[1024,10,256]{2,0,1:T(8,128)}), f32[128,10,256]{2,0,1:T(8,128)}) %reduce-scatter.24.cloned.1.call-update) | async-done | bytes 1310736 | tf_op jit(solution)/shard_map/reduce_scatter | solution.py:38
  871.2 34.7 %reduce-scatter.26.cloned.1.call-done = f32[128,256]{1,0:T(8,128)} async-done(((f32[1024,256]{1,0:T(8,128)}), f32[128,256]{1,0:T(8,128)}) %reduce-scatter.26.cloned.1.call-update) | async-done | bytes 131088 | tf_op jit(solution)/shard_map/reduce_scatter | solution.py:39
  (101 shorter events, 51.9 us)
Async XLA Ops:
  6.5 43.1 %all-gather.7.cloned.1.call-start = ((), (), s32[]{:S(2)}) async-start(), calls=%async_computation.9 | async-start | bytes 4718592 | tf_op jit(solution)/shard_map/all_gather | solution.py:26
  7.5 2.8 copy-start.5
  10.2 86.7 %all-gather.9.cloned.1.call-start = ((), (), s32[]{:S(2)}) async-start(), calls=%async_computation.11 | async-start | bytes 2621440 | tf_op jit(solution)/shard_map/all_gather | solution.py:30
  12.6 162.3 %reduce-scatter.10.cloned.1.call-start = ((), (), s32[]{:S(2)}) async-start(), calls=%async_computation.10 | async-start | bytes 5242880 | tf_op jit(solution)/shard_map/reduce_scatter | solution.py:33
  69.1 181.0 %reduce-scatter.12.cloned.1.call-start = ((), (), s32[]{:S(2)}) async-start(), calls=%async_computation.12 | async-start | bytes 9437184 | tf_op jit(solution)/shard_map/reduce_scatter | solution.py:38
  115.5 59.3 %copy-start.3 = (bf16[8,128,1024]{1,2,0:T(8,128)(2,1)S(1)}, bf16[8,128,1024]{1,2,0:T(8,128)(2,1)}, u32[]{:S(2)}) copy-start(bf16[8,128,1024]{1,2,0:T(8,128)(2,1)} %all-gather.9.cloned.1.call-done) | copy-start | bytes 6291460
  115.6 173.6 %reduce-scatter.14.cloned.1.call-start = ((), (), s32[]{:S(2)}) async-start(), calls=%async_computation.13 | async-start | bytes 1179648 | tf_op jit(solution)/shard_map/reduce_scatter | solution.py:39
  179.0 150.7 %all-gather.11.cloned.1.call-start = ((), (), s32[]{:S(2)}) async-start(), calls=%async_computation.14 | async-start | bytes 5308416 | tf_op jit(solution)/shard_map/all_gather | solution.py:26
  180.8 200.5 %all-gather.13.cloned.1.call-start = ((), (), s32[]{:S(2)}) async-start(), calls=%async_computation.16 | async-start | bytes 2949120 | tf_op jit(solution)/shard_map/all_gather | solution.py:30
  184.0 283.7 %reduce-scatter.16.cloned.1.call-start = ((), (), s32[]{:S(2)}) async-start(), calls=%async_computation.15 | async-start | bytes 5898240 | tf_op jit(solution)/shard_map/reduce_scatter | solution.py:33
  191.8 6.4 copy-start.2
  198.2 90.9 %copy-start.4 = (f32[3,128,256]{2,1,0:T(8,128)S(1)}, f32[3,128,256]{2,1,0:T(8,128)}, u32[]{:S(2)}) copy-start(f32[3,128,256]{2,1,0:T(8,128)} %param.28) | copy-start | bytes 1179652
  351.3 197.0 %reduce-scatter.18.cloned.1.call-start = ((), (), s32[]{:S(2)}) async-start(), calls=%async_computation.17 | async-start | bytes 10616832 | tf_op jit(solution)/shard_map/reduce_scatter | solution.py:38
  404.8 182.5 %reduce-scatter.20.cloned.1.call-start = ((), (), s32[]{:S(2)}) async-start(), calls=%async_computation.18 | async-start | bytes 1179648 | tf_op jit(solution)/shard_map/reduce_scatter | solution.py:39
  467.6 11.4 %copy-start.1 = (f32[9,128,256]{2,1,0:T(8,128)S(1)}, f32[9,128,256]{2,1,0:T(8,128)}, u32[]{:S(2)}) copy-start(f32[9,128,256]{2,1,0:T(8,128)} %reduce-scatter.16.cloned.1.call-done) | copy-start | bytes 3538948
  473.1 157.1 %all-gather.15.cloned.1.call-start = ((), (), s32[]{:S(2)}) async-start(), calls=%async_computation.19 | async-start | bytes 5898240 | tf_op jit(solution)/shard_map/all_gather | solution.py:26
  474.9 211.5 %all-gather.17.cloned.1.call-start = ((), (), s32[]{:S(2)}) async-start(), calls=%async_computation.21 | async-start | bytes 3276800 | tf_op jit(solution)/shard_map/all_gather | solution.py:30
  478.1 303.2 %reduce-scatter.22.cloned.1.call-start = ((), (), s32[]{:S(2)}) async-start(), calls=%async_computation.20 | async-start | bytes 6553600 | tf_op jit(solution)/shard_map/reduce_scatter | solution.py:33
  655.9 211.0 %reduce-scatter.24.cloned.1.call-start = ((), (), s32[]{:S(2)}) async-start(), calls=%async_computation.22 | async-start | bytes 11796480 | tf_op jit(solution)/shard_map/reduce_scatter | solution.py:38
  716.3 72.1 %copy-start.6 = (s32[4]{0:T(128)S(1)}, s32[4]{0:T(128)}, u32[]{:S(2)}) copy-start(s32[4]{0:T(128)} %constant.314.clone.1) | copy-start | bytes 52
  716.3 189.6 %reduce-scatter.26.cloned.1.call-start = ((), (), s32[]{:S(2)}) async-start(), calls=%async_computation.23 | async-start | bytes 1179648 | tf_op jit(solution)/shard_map/reduce_scatter | solution.py:39
  781.3 8.5 copy-start
Sparse Core Ops, SparseCore 0:
  10.3 39.2 all-gather.6
  51.2 45.6 all-gather.8
  99.2 75.5 reduce-scatter.9
  178.2 71.8 reduce-scatter.11
  253.1 35.9 reduce-scatter.13
  290.9 38.7 all-gather.10
  331.3 49.9 all-gather.12
  383.6 84.0 reduce-scatter.15
  471.1 77.1 reduce-scatter.17
  551.3 35.9 reduce-scatter.19
  589.2 40.9 all-gather.14
  631.7 54.7 all-gather.16
  688.7 92.5 reduce-scatter.21
  784.7 82.1 reduce-scatter.23
  869.9 35.9 reduce-scatter.25
where the time goes:
time: 921 us; the launch traced here: 914 us
  waiting for transfers between devices  692 us (75%)
  matrix products  154 us (17%)
  other arithmetic  28.7 us (3%)
  local copies, waits for them, and re-layouts  24.8 us (3%)
  between operations  13.9 us (2%)
    reduce_scatter x3, waiting for transfers between devices, per_device(): lax.psum_scatter(row_terms, 'col', scatter_dimension=0, tiled=True)  194 us
    reduce_scatter x3, waiting for transfers between devices, per_device(): lax.psum_scatter(col_terms, 'row', scatter_dimension=2, tiled=True)  184 us
    all_gather x3, waiting for transfers between devices, per_device(): lax.all_gather(lower, 'col', axis=0, tiled=True).astype(jnp.float32)  117 us
    reduce_scatter x3, waiting for transfers between devices, per_device(): lax.psum_scatter(diag_terms, 'col', scatter_dimension=0, tiled=True)  108 us
    all_gather x3, waiting for transfers between devices, per_device(): lax.all_gather(upper, 'row', axis=2, tiled=True).astype(jnp.float32)  87.2 us
    dot_general x3, matrix products, per_device(): jnp.einsum('akw,akbj->wbj', upper_full, known, precision=lax.Precision.HI...  72 us
    dot_general x3, matrix products, per_device(): jnp.einsum('ajbk,wbk->ajw', known, lower_full, precision=lax.Precision.HI...  66.7 us
  transfers between devices with their start and end apart: 15, of which 15 were waited for; matrix products, arithmetic and copies ran while one was open for 22% of the time, Pallas kernels for 0%

commit v1 on v0

v1 whole, which is shorter than its diff:
```python
import jax
import jax.numpy as jnp
from jax import lax
from jax.sharding import PartitionSpec as P

BLK = 128
NSUP = 3
NSEG = 11


def split(x):
    hi = lax.reduce_precision(x, 8, 7)
    return hi.astype(jnp.bfloat16), (x - hi).astype(jnp.bfloat16)


def two_pass(spec, first, second, wide_first):
    out = None
    for part in first if wide_first else second:
        args = (part, second) if wide_first else (first, part)
        term = jnp.einsum(spec, *args, preferred_element_type=jnp.float32)
        out = term if out is None else out + term
    return out


def scatter_sum(terms, axis, n):
    parts = terms.reshape((n, terms.shape[0] // n) + terms.shape[1:])
    return jnp.sum(lax.all_to_all(parts, axis, 0, 0), axis=0)


def per_device(n_col, region, l_panels, u_panels, diag_inv, pattern):
    rows_here = region.shape[1]
    cols_here = region.shape[3]
    row_index = lax.axis_index("row")
    col_index = lax.axis_index("col")
    block_mask = jnp.repeat(pattern.astype(jnp.float32), BLK, axis=2)
    mask_rows = lax.dynamic_slice_in_dim(block_mask, col_index * rows_here, rows_here, 2)
    mask_cols = lax.dynamic_slice_in_dim(block_mask, row_index * cols_here, cols_here, 2)
    inverse = jnp.zeros((NSEG, rows_here, NSEG, cols_here), jnp.float32)
    inverse = inverse.at[NSUP:, :, NSUP:, :].set(region)
    lowers, uppers = {}, {}
    for level in reversed(range(NSUP)):
        start = level + 1
        lower = l_panels[level][:, start:, :] * mask_cols[level, None, start:, :].astype(jnp.bfloat16)
        upper = u_panels[level][start:] * mask_rows[level, start:, :, None].astype(jnp.bfloat16)
        lowers[level] = lax.all_gather(lower, "col", axis=0, tiled=True)
        uppers[level] = lax.all_gather(upper, "row", axis=2, tiled=True)
    for level in reversed(range(NSUP)):
        start = level + 1
        lower, upper = lowers[level], uppers[level]
        known = split(inverse[start:, :, start:, :])
        col_terms = two_pass("ajbk,wbk->ajw", known, lower, True)
        col_sum = lax.psum_scatter(col_terms, "row", scatter_dimension=2, tiled=True)
        row_terms = two_pass("akw,akbj->wbj", upper, known, False)
        row_sum = scatter_sum(row_terms, "col", n_col)
        row_panel = -mask_cols[level, None, start:, :] * row_sum
        column = -mask_rows[level, start:, :, None] * col_sum
        diag_terms = two_pass("akw,akv->wv", upper, split(column), False)
        diagonal = diag_inv[level] - scatter_sum(diag_terms, "col", n_col)
        inverse = inverse.at[start:, :, level, :].set(column)
        inverse = inverse.at[level, :, start:, :].set(row_panel)
        inverse = inverse.at[level, :, level, :].set(diagonal)
    return inverse


def solution(mesh):
    in_specs = (
        P(None, "col", None, "row"),
        P(None, "col", None, "row"),
        P(None, None, "col", "row"),
        P(None, "col", "row"),
        P(),
    )
    out_specs = P(None, "col", None, "row")
    n_col = mesh.shape["col"]

    def body(*args):
        return per_device(n_col, *args)

    return jax.shard_map(
        body, mesh=mesh, in_specs=in_specs, out_specs=out_specs, check_vma=False
    )
```

time: 921 us -> 702 us (0.76)
  waiting for transfers between devices: 692 us -> 420 us
  starting transfers between devices: 1.69 us -> 39.5 us
  other arithmetic: 28.7 us -> 48.8 us
  matrix products: 154 us -> 137 us
  local copies, waits for them, and re-layouts: 24.8 us -> 39.6 us
    reduce_scatter x6 -> x0, waiting for transfers between devices: 302 us -> none  [the longest x3 194 us: per_device(): lax.psum_scatter(row_terms, 'col', scatter_dimension=0, tiled=True)]
    all_to_all x0 -> x6, waiting for transfers between devices: none -> 194 us  [scatter_sum(): return jnp.sum(lax.all_to_all(parts, axis, 0, 0), axis=0)]
    all_gather x6, waiting for transfers between devices: 205 us -> 76.1 us  [the longest x3 47.4 us: per_device(): uppers[level] = lax.all_gather(upper, 'row', axis=2, tiled=True)]
    all_to_all x0 -> x6, starting transfers between devices: none -> 39 us  [scatter_sum(): return jnp.sum(lax.all_to_all(parts, axis, 0, 0), axis=0)]
    reduce_scatter x3, waiting for transfers between devices: 184 us -> 150 us  [per_device(): lax.psum_scatter(col_terms, 'row', scatter_dimension=2, tiled=True)]
    dot_general x9 -> x18, matrix products: 154 us -> 137 us  [two_pass(): term = jnp.einsum(spec, *args, preferred_element_type=jnp.float32)]
    reduce_sum x0 -> x6, other arithmetic: none -> 14.9 us  [scatter_sum(): return jnp.sum(lax.all_to_all(parts, axis, 0, 0), axis=0)]
    reshape x0 -> x3, local copies, waits for them, and re-layouts: none -> 13.3 us  [scatter_sum(): parts = terms.reshape((n, terms.shape[0] // n) + terms.shape[1:])]
  transfers between devices with their start and end apart: 15 -> 15, of which waited for: 15 -> 12; matrix products, arithmetic and copies ran while one was open for 22% -> 31% of each run, Pallas kernels for 0% -> 0%
where the time goes in v1:
time: 702 us; the launch traced here: 699 us
  waiting for transfers between devices  420 us (60%)
  matrix products  137 us (20%)
  other arithmetic  48.8 us (7%)
  local copies, waits for them, and re-layouts  39.6 us (6%)
  starting transfers between devices  39.5 us (6%)
  between operations  14.1 us (2%)
    all_to_all x6, waiting for transfers between devices, scatter_sum(): return jnp.sum(lax.all_to_all(parts, axis, 0, 0), axis=0)  194 us
    reduce_scatter x3, waiting for transfers between devices, per_device(): lax.psum_scatter(col_terms, 'row', scatter_dimension=2, tiled=True)  150 us
    dot_general x18, matrix products, two_pass(): term = jnp.einsum(spec, *args, preferred_element_type=jnp.float32)  137 us
    all_gather x3, waiting for transfers between devices, per_device(): uppers[level] = lax.all_gather(upper, 'row', axis=2, tiled=True)  47.4 us
    all_to_all x6, starting transfers between devices, scatter_sum(): return jnp.sum(lax.all_to_all(parts, axis, 0, 0), axis=0)  39 us
    all_gather x3, waiting for transfers between devices, per_device(): lowers[level] = lax.all_gather(lower, 'col', axis=0, tiled=True)  28.8 us
    reduce_sum x6, other arithmetic, scatter_sum(): return jnp.sum(lax.all_to_all(parts, axis, 0, 0), axis=0)  14.9 us
  transfers between devices with their start and end apart: 15, of which 12 were waited for; matrix products, arithmetic and copies ran while one was open for 31% of the time, Pallas kernels for 0%

profile of v1, /device:TPU:0, one launch (start us, length us, event | category | flops | bytes accessed | tf_op | source)
XLA Modules:
  0.0 698.7 jit_solution(3894948132041312491)
XLA Ops:
  13.5 8.3 %reduce-precision_convert_fusion.2 = (bf16[8,128,8,256]{3,2,1,0:T(8,128)(2,1)}, bf16[8,128,8,256]{3,2,1,0:T(8,128)(2,1)}) fusion(f32[8,128,8,256]{3,2,1,0:T(8,128)} %param.25), kind=kLoop, calls=%fused_computation.6 | loop fusion | flops 8388608 | bytes 16777216 | tf_op jit(solution)/shard_map/convert_element_type | solution.py:13
  21.8 28.8 %all-gather.7.cloned.1.call-done = bf16[1024,8,256]{2,0,1:T(8,128)(2,1)} async-done(((bf16[128,8,256]{2,0,1:T(8,128)(2,1)}), bf16[1024,8,256]{2,0,1:T(8,128)(2,1)}) %all-gather.7.cloned.1.call-update) | async-done | bytes 4194320 | tf_op jit(solution)/shard_map/all_gather | solution.py:45
  50.5 8.1 %fusion.11 = f32[8,128,1024,1]{1,2,3,0:T(8,128)S(1)} fusion(bf16[1024,8,256]{2,0,1:T(8,128)(2,1)} %all-gather.7.cloned.1.call-done, bf16[8,128,8,256]{3,2,1,0:T(8,128)(2,1)} %get-tuple-element.126), kind=kOutput, calls=%fused_computation.23 | convolution fusion | flops 4294967296 | bytes 12582912 | tf_op jit(solution)/shard_map/ajbk,wbk->ajw/dot_general | solution.py:20
  58.6 6.1 bitcast_add_fusion.5
  65.8 32.0 %all-gather.9.cloned.1.call-done = bf16[8,128,1024]{1,2,0:T(8,128)(2,1)} async-done(((bf16[8,128,256]{1,2,0:T(8,128)(2,1)}), bf16[8,128,1024]{1,2,0:T(8,128)(2,1)}) %all-gather.9.cloned.1.call-update) | async-done | bytes 2097168 | tf_op jit(solution)/shard_map/all_gather | solution.py:46
  97.8 7.2 %fusion.15 = f32[1024,8,256,1]{2,0,3,1:T(8,128)S(1)} fusion(bf16[8,128,8,256]{3,2,1,0:T(8,128)(2,1)} %get-tuple-element.126, bf16[8,128,1024]{1,2,0:T(8,128)(2,1)} %all-gather.9.cloned.1.call-done), kind=kOutput, calls=%fused_computation.27 | convolution fusion | flops 4294967296 | bytes 14680064 | tf_op jit(solution)/shard_map/akw,akbj->wbj/dot_general | solution.py:20
  113.5 17.1 %all-to-all-start = ((f32[8,128,8,256]{3,1,2,0:T(8,128)}), f32[8,128,8,256]{3,1,2,0:T(8,128)}, u32[]{:S(2)}, u32[]{:S(2)}) async-start(f32[8,128,8,256]{3,1,2,0:T(8,128)} %copy.66), calls=%async_computation.1 | async-start | bytes 16777216 | tf_op jit(solution)/shard_map/all_to_all | solution.py:27
  132.2 43.5 %reduce-scatter.4.cloned.1.call-done = f32[8,128,256]{1,2,0:T(8,128)} async-done(((f32[8,128,1024]{1,2,0:T(8,128)}), f32[8,128,256]{1,2,0:T(8,128)}) %reduce-scatter.4.cloned.1.call-update) | async-done | bytes 1048592 | tf_op jit(solution)/shard_map/reduce_scatter | solution.py:52
  179.5 62.3 %all-to-all-done = f32[8,128,8,256]{3,1,2,0:T(8,128)} async-done(((f32[8,128,8,256]{3,1,2,0:T(8,128)}), f32[8,128,8,256]{3,1,2,0:T(8,128)}, u32[]{:S(2)}, u32[]{:S(2)}) %all-to-all-start) | async-done | bytes 8388640 | tf_op jit(solution)/shard_map/all_to_all | solution.py:27
  246.4 5.9 copy.57
  252.4 6.2 scatter.34
  270.4 12.3 %fusion.7 = f32[9,128,1024,1]{2,1,3,0:T(8,128)} fusion(bf16[1024,9,256]{2,0,1:T(8,128)(2,1)} %all-gather.11.cloned.1.call-done, f32[11,128,11,256]{3,1,2,0:T(8,128)} %fusion.64), kind=kOutput, calls=%fused_computation.18 | convolution fusion | flops 5443780608 | bytes 20054016 | tf_op jit(solution)/shard_map/ajbk,wbk->ajw/dot_general | solution.py:20
  283.5 9.1 %bitcast_add_fusion.4 = f32[9,128,1024]{2,1,0:T(8,128)} fusion(f32[9,128,1024,1]{2,1,3,0:T(8,128)} %fusion.7, bf16[1024,9,256]{2,0,1:T(8,128)(2,1)S(1)} %copy-done.14, f32[11,128,11,256]{3,1,2,0:T(8,128)S(1)} %copy-done), kind=kOutput, calls=%fused_computation.17 | convolution fusion | flops 5442306048 | bytes 24772608 | tf_op jit(solution)/shard_map/ajbk,wbk->ajw/dot_general | solution.py:20
  296.1 13.5 %fusion.29 = f32[1024,9,256,1]{2,0,1,3:T(8,128)} fusion(bf16[9,128,1024]{1,2,0:T(8,128)(2,1)} %all-gather.13.cloned.1.call-done, f32[11,128,11,256]{3,1,2,0:T(8,128)} %fusion.64), kind=kOutput, calls=%fused_computation.37 | convolution fusion | flops 5441126400 | bytes 22413312 | tf_op jit(solution)/shard_map/akw,akbj->wbj/dot_general | solution.py:20
  309.6 10.4 %bitcast_add_fusion.1 = f32[1024,9,256]{2,0,1:T(8,128)S(1)} fusion(f32[1024,9,256,1]{2,0,1,3:T(8,128)} %fusion.29, bf16[9,128,1024]{1,2,0:T(8,128)(2,1)S(1)} %copy-done.3, f32[11,128,11,256]{3,1,2,0:T(8,128)} %fusion.64), kind=kOutput, calls=%fused_computation.9 | convolution fusion | flops 5446139904 | bytes 31850496 | tf_op jit(solution)/shard_map/akw,akbj->wbj/dot_general | solution.py:20
  332.2 50.1 %reduce-scatter.6.cloned.1.call-done = f32[9,128,256]{2,1,0:T(8,128)} async-done(((f32[9,128,1024]{2,1,0:T(8,128)}), f32[9,128,256]{2,1,0:T(8,128)}) %reduce-scatter.6.cloned.1.call-update) | async-done | bytes 1179664 | tf_op jit(solution)/shard_map/reduce_scatter | solution.py:52
  386.7 68.7 %all-to-all-done.2 = f32[8,128,9,256]{3,1,2,0:T(8,128)} async-done(((f32[8,128,9,256]{3,1,2,0:T(8,128)}), f32[8,128,9,256]{3,1,2,0:T(8,128)}, u32[]{:S(2)}, u32[]{:S(2)}) %all-to-all-start.2) | async-done | bytes 9437216 | tf_op jit(solution)/shard_map/all_to_all | solution.py:27
  476.0 13.2 %fusion.3 = f32[10,128,1024,1]{2,1,3,0:T(8,128)} fusion(bf16[1024,10,256]{2,0,1:T(8,128)(2,1)} %all-gather.15.cloned.1.call-done, f32[11,128,11,256]{3,1,2,0:T(8,128)} %fusion.63), kind=kOutput, calls=%fused_computation.13 | convolution fusion | flops 6720716800 | bytes 23592960 | tf_op jit(solution)/shard_map/ajbk,wbk->ajw/dot_general | solution.py:20
  489.2 11.6 %bitcast_add_fusion.3 = f32[10,128,1024]{2,1,0:T(8,128)} fusion(f32[10,128,1024,1]{2,1,3,0:T(8,128)} %fusion.3, bf16[1024,10,256]{2,0,1:T(8,128)(2,1)} %all-gather.15.cloned.1.call-done, f32[11,128,11,256]{3,1,2,0:T(8,128)S(1)} %copy-done.1), kind=kOutput, calls=%fused_computation.12 | convolution fusion | flops 6718750720 | bytes 28835840 | tf_op jit(solution)/shard_map/ajbk,wbk->ajw/dot_general | solution.py:20
  500.9 13.9 %all-gather.17.cloned.1.call-done = bf16[10,128,1024]{1,2,0:T(8,128)(2,1)} async-done(((bf16[10,128,256]{1,2,0:T(8,128)(2,1)}), bf16[10,128,1024]{1,2,0:T(8,128)(2,1)}) %all-gather.17.cloned.1.call-update) | async-done | bytes 2621456 | tf_op jit(solution)/shard_map/all_gather | solution.py:46
  514.8 15.5 %fusion.24 = f32[1024,10,256,1]{2,0,1,3:T(8,128)} fusion(bf16[10,128,1024]{1,2,0:T(8,128)(2,1)} %all-gather.17.cloned.1.call-done, f32[11,128,11,256]{3,1,2,0:T(8,128)} %fusion.63), kind=kOutput, calls=%fused_computation.34 | convolution fusion | flops 6717440000 | bytes 26214400 | tf_op jit(solution)/shard_map/akw,akbj->wbj/dot_general | solution.py:20
  530.3 12.4 %bitcast_add_fusion = f32[1024,10,256]{2,0,1:T(8,128)S(1)} fusion(f32[1024,10,256,1]{2,0,1,3:T(8,128)} %fusion.24, bf16[10,128,1024]{1,2,0:T(8,128)(2,1)S(1)} %copy-done.2, f32[11,128,11,256]{3,1,2,0:T(8,128)} %fusion.63), kind=kOutput, calls=%fused_computation.8 | convolution fusion | flops 6723338240 | bytes 36700160 | tf_op jit(solution)/shard_map/akw,akbj->wbj/dot_general | solution.py:20
  553.5 56.2 %reduce-scatter.8.cloned.1.call-done = f32[10,128,256]{2,1,0:T(8,128)} async-done(((f32[10,128,1024]{2,1,0:T(8,128)}), f32[10,128,256]{2,1,0:T(8,128)}) %reduce-scatter.8.cloned.1.call-update) | async-done | bytes 1310736 | tf_op jit(solution)/shard_map/reduce_scatter | solution.py:52
  614.0 55.2 %all-to-all-done.4 = f32[8,128,10,256]{3,1,2,0:T(8,128)} async-done(((f32[8,128,10,256]{3,1,2,0:T(8,128)}), f32[8,128,10,256]{3,1,2,0:T(8,128)}, u32[]{:S(2)}, u32[]{:S(2)}) %all-to-all-start.4) | async-done | bytes 10485792 | tf_op jit(solution)/shard_map/all_to_all | solution.py:27
  (132 shorter events, 117.0 us)
Async XLA Ops:
  6.5 44.0 %all-gather.7.cloned.1.call-start = ((), (), s32[]{:S(2)}) async-start(), calls=%async_computation.9 | async-start | bytes 4718592 | tf_op jit(solution)/shard_map/all_gather | solution.py:45
  7.5 323.6 %copy-start.12 = (f32[3,11,1024]{2,0,1:T(4,128)}, f32[3,11,1024]{2,0,1:T(4,128)S(1)}, u32[]{:S(2)}) copy-start(f32[3,11,1024]{2,0,1:T(4,128)S(1)} %reshape.505) | copy-start | bytes 405508
  11.1 86.7 %all-gather.9.cloned.1.call-start = ((), (), s32[]{:S(2)}) async-start(), calls=%async_computation.11 | async-start | bytes 2621440 | tf_op jit(solution)/shard_map/all_gather | solution.py:46
  13.5 162.2 %reduce-scatter.4.cloned.1.call-start = ((), (), s32[]{:S(2)}) async-start(), calls=%async_computation.10 | async-start | bytes 5242880 | tf_op jit(solution)/shard_map/reduce_scatter | solution.py:52
  50.5 8.1 %copy-start.8 = (bf16[8,128,8,256]{3,2,1,0:T(8,128)(2,1)S(1)}, bf16[8,128,8,256]{3,2,1,0:T(8,128)(2,1)}, u32[]{:S(2)}) copy-start(bf16[8,128,8,256]{3,2,1,0:T(8,128)(2,1)} %get-tuple-element.125) | copy-start | bytes 12582916
  50.5 8.1 %copy-start.15 = (bf16[1024,8,256]{2,0,1:T(8,128)(2,1)S(1)}, bf16[1024,8,256]{2,0,1:T(8,128)(2,1)}, u32[]{:S(2)}) copy-start(bf16[1024,8,256]{2,0,1:T(8,128)(2,1)} %all-gather.7.cloned.1.call-done) | copy-start | bytes 12582916
  64.7 205.7 %all-gather.11.cloned.1.call-start = ((), (), s32[]{:S(2)}) async-start(), calls=%async_computation.12 | async-start | bytes 5308416 | tf_op jit(solution)/shard_map/all_gather | solution.py:45
  113.5 128.4 %all-to-all-start = ((f32[8,128,8,256]{3,1,2,0:T(8,128)}), f32[8,128,8,256]{3,1,2,0:T(8,128)}, u32[]{:S(2)}, u32[]{:S(2)}) async-start(f32[8,128,8,256]{3,1,2,0:T(8,128)} %copy.66), calls=%async_computation.1 | async-start | bytes 16777216 | tf_op jit(solution)/shard_map/all_to_all | solution.py:27
  241.9 26.9 %all-to-all-start.1 = ((f32[8,128,256]{2,1,0:T(8,128)}), f32[8,128,256]{2,1,0:T(8,128)S(1)}, u32[]{:S(2)}, u32[]{:S(2)}) async-start(f32[8,128,256]{2,1,0:T(8,128)} %bitcast.19), calls=%async_computation.2 | async-start | bytes 2097152 | tf_op jit(solution)/shard_map/all_to_all | solution.py:27
  245.4 50.7 %all-gather.13.cloned.1.call-start = ((), (), s32[]{:S(2)}) async-start(), calls=%async_computation.14 | async-start | bytes 2949120 | tf_op jit(solution)/shard_map/all_gather | solution.py:46
  246.4 136.0 %reduce-scatter.6.cloned.1.call-start = ((), (), s32[]{:S(2)}) async-start(), calls=%async_computation.13 | async-start | bytes 5898240 | tf_op jit(solution)/shard_map/reduce_scatter | solution.py:52
  270.4 12.3 %copy-start = (f32[11,128,11,256]{3,1,2,0:T(8,128)S(1)}, f32[11,128,11,256]{3,1,2,0:T(8,128)}, u32[]{:S(2)}) copy-start(f32[11,128,11,256]{3,1,2,0:T(8,128)} %fusion.64) | copy-start | bytes 47579140
  270.4 13.1 %copy-start.14 = (bf16[1024,9,256]{2,0,1:T(8,128)(2,1)S(1)}, bf16[1024,9,256]{2,0,1:T(8,128)(2,1)}, u32[]{:S(2)}) copy-start(bf16[1024,9,256]{2,0,1:T(8,128)(2,1)} %all-gather.11.cloned.1.call-done) | copy-start | bytes 14155780
  292.6 183.3 %all-gather.15.cloned.1.call-start = ((), (), s32[]{:S(2)}) async-start(), calls=%async_computation.15 | async-start | bytes 5898240 | tf_op jit(solution)/shard_map/all_gather | solution.py:45
  296.1 13.5 %copy-start.3 = (bf16[9,128,1024]{1,2,0:T(8,128)(2,1)S(1)}, bf16[9,128,1024]{1,2,0:T(8,128)(2,1)}, u32[]{:S(2)}) copy-start(bf16[9,128,1024]{1,2,0:T(8,128)(2,1)} %all-gather.13.cloned.1.call-done) | copy-start | bytes 7077892
  324.8 130.7 %all-to-all-start.2 = ((f32[8,128,9,256]{3,1,2,0:T(8,128)}), f32[8,128,9,256]{3,1,2,0:T(8,128)}, u32[]{:S(2)}, u32[]{:S(2)}) async-start(f32[8,128,9,256]{3,1,2,0:T(8,128)} %copy.72), calls=%async_computation.4 | async-start | bytes 18874368 | tf_op jit(solution)/shard_map/all_to_all | solution.py:27
  455.4 18.9 %all-to-all-start.3 = ((f32[8,128,256]{2,1,0:T(8,128)}), f32[8,128,256]{2,1,0:T(8,128)S(1)}, u32[]{:S(2)}, u32[]{:S(2)}) async-start(f32[8,128,256]{2,1,0:T(8,128)} %bitcast.39), calls=%async_computation.5 | async-start | bytes 2097152 | tf_op jit(solution)/shard_map/all_to_all | solution.py:27
  459.0 55.8 %all-gather.17.cloned.1.call-start = ((), (), s32[]{:S(2)}) async-start(), calls=%async_computation.17 | async-start | bytes 3276800 | tf_op jit(solution)/shard_map/all_gather | solution.py:46
  461.0 148.6 %reduce-scatter.8.cloned.1.call-start = ((), (), s32[]{:S(2)}) async-start(), calls=%async_computation.16 | async-start | bytes 6553600 | tf_op jit(solution)/shard_map/reduce_scatter | solution.py:52
  476.0 13.2 %copy-start.1 = (f32[11,128,11,256]{3,1,2,0:T(8,128)S(1)}, f32[11,128,11,256]{3,1,2,0:T(8,128)}, u32[]{:S(2)}) copy-start(f32[11,128,11,256]{3,1,2,0:T(8,128)} %fusion.63) | copy-start | bytes 47579140
  514.8 15.5 %copy-start.2 = (bf16[10,128,1024]{1,2,0:T(8,128)(2,1)S(1)}, bf16[10,128,1024]{1,2,0:T(8,128)(2,1)}, u32[]{:S(2)}) copy-start(bf16[10,128,1024]{1,2,0:T(8,128)(2,1)} %all-gather.17.cloned.1.call-done) | copy-start | bytes 7864324
  547.3 121.9 %all-to-all-start.4 = ((f32[8,128,10,256]{3,1,2,0:T(8,128)}), f32[8,128,10,256]{3,1,2,0:T(8,128)}, u32[]{:S(2)}, u32[]{:S(2)}) async-start(f32[8,128,10,256]{3,1,2,0:T(8,128)} %copy.76), calls=%async_computation.7 | async-start | bytes 20971520 | tf_op jit(solution)/shard_map/all_to_all | solution.py:27
  612.1 62.8 %copy-start.13 = (s32[4]{0:T(128)S(1)}, s32[4]{0:T(128)}, u32[]{:S(2)}) copy-start(s32[4]{0:T(128)} %constant.315.clone.1) | copy-start | bytes 52
  669.2 19.6 %all-to-all-start.5 = ((f32[8,128,256]{2,1,0:T(8,128)}), f32[8,128,256]{2,1,0:T(8,128)}, u32[]{:S(2)}, u32[]{:S(2)}) async-start(f32[8,128,256]{2,1,0:T(8,128)} %bitcast.211), calls=%async_computation.8 | async-start | bytes 2097152 | tf_op jit(solution)/shard_map/all_to_all | solution.py:27
  (7 other events, 27.2 us)
Sparse Core Ops, SparseCore 0:
  11.2 39.2 all-gather.6
  52.1 45.6 all-gather.8
  100.1 75.5 reduce-scatter.3
  177.5 67.7 all-gather.10
  247.5 48.5 all-gather.12
  298.3 84.0 reduce-scatter.5
  384.2 73.5 all-gather.14
  461.4 53.3 all-gather.16
  517.1 92.5 reduce-scatter.7
